TPU v7x, 512 devices: a whole 4x4x16 slice. The times are simulated.
512 devices in a mesh: seq: 64 (over z, y), tp: 8 (over x, core).
Axes of the slice: x: 4, y: 4, z: 16, core: 2. Of those that a mesh axis runs over, the one named last changes fastest.
Arguments:
- residual: bfloat16 [8192, 8192], P('seq', 'tp'), may hold values from -6 to 6
- steer_table: bfloat16 [7, 8192], P(None, 'tp'), may hold values from -6 to 6
- steer_index: int32 [4], replicated, may hold values from 0 to 6
- steer_num: int32 [4], replicated, may hold values from -8 to 8
- lengths: int32 [4], replicated, may hold values from 1 to 4096, 8192 in all
- queries: bfloat16 [8192, 64, 128], P('seq', 'tp'), may hold values from -128 to 128
- keys: bfloat16 [8192, 8, 128], P('seq', 'tp'), may hold values from -6 to 6
- values: bfloat16 [8192, 8, 128], P('seq', 'tp'), may hold values from -6 to 6
- inner_x: bfloat16 [8192, 16384], P('seq', 'tp'), may hold values from -6 to 6
- dt_raw: bfloat16 [8192, 16384], P('seq', 'tp'), may hold values from -4 to 4
- dt_bias: float32 [16384], P('tp'), may hold values from -7 to -2.5
- a_log: float32 [16, 16384], P(None, 'tp'), may hold values from -2.3 to 2.77
- skip_gain: float32 [16384], P('tp'), may hold values from 0.5 to 1.5
- bc_weight: bfloat16 [32, 16384], P(None, 'tp'), may hold values from -0.046875 to 0.046875
Outputs:
- steered: bfloat16 [8192, 8192], P('seq', 'tp')
- context: bfloat16 [8192, 64, 128], P('seq', 'tp')
- mixed: bfloat16 [8192, 16384], P('seq', 'tp')
Inputs may be any that keep to these rules, and one draw needn't show every extreme that they name: `lengths`: the 4 requests lie end to end in token order and the longest has exactly 8192 // 2 tokens. `steer_num`: a request's steering multiplier is its numerator over 4.
All inputs are finite; a program needn't handle non-finite values.
Results may differ from a plain program's by a relative error of at most 0.0039.
Values may be sent and summed in bfloat16 or wider, within the bound.
A program may use at most 128 MiB of HBM per device.

v0:
```python
import jax
import jax.numpy as jnp
from jax import lax
from jax.sharding import PartitionSpec as P

NEG_FILL = -1e30
KEY_BLOCK = 512


def prefix(part, axis, combine, identity):
    place = lax.axis_index(axis)
    gathered = jax.tree.map(lambda a: lax.all_gather(a, axis), part)
    state = jax.tree.map(lambda a, e: jnp.zeros_like(a) + jnp.asarray(e, a.dtype), part, identity)

    def one(lap, state):
        return combine(
            state, jax.tree.map(lambda a: lax.dynamic_index_in_dim(a, lap, 0, False), gathered)
        )

    return lax.fori_loop(0, place, one, state)


def request_bounds(lengths, positions):
    seg_ends = jnp.cumsum(lengths)
    seg_starts = seg_ends - lengths
    member = (positions[:, None] >= seg_starts[None, :]) & (positions[:, None] < seg_ends[None, :])
    member_int = member.astype(jnp.int32)
    req_start = jnp.sum(member_int * seg_starts[None, :], axis=1)
    return (member_int, req_start)


def chain_combine(earlier, later):
    return (earlier[0] * later[0], later[0] * earlier[1] + later[1])


def shards(
    residual,
    steer_table,
    steer_index,
    steer_num,
    lengths,
    queries,
    keys,
    values,
    inner_x,
    dt_raw,
    dt_bias,
    a_log,
    skip_gain,
    bc_weight,
):
    tok_rows = residual.shape[0]
    positions = lax.axis_index("seq") * tok_rows + jnp.arange(tok_rows, dtype=jnp.int32)
    member_int, req_start = request_bounds(lengths, positions)
    vector_pick = (
        steer_index[:, None] == jnp.arange(steer_table.shape[0], dtype=jnp.int32)[None, :]
    ).astype(jnp.float32)
    vector_pick = vector_pick * (steer_num.astype(jnp.float32) * 0.25)[:, None]
    token_pick = jnp.dot(
        member_int.astype(jnp.float32), vector_pick, precision=lax.Precision.HIGHEST
    )
    steer_add = jnp.dot(
        token_pick, steer_table.astype(jnp.float32), precision=lax.Precision.HIGHEST
    )
    steered = (residual.astype(jnp.float32) + steer_add).astype(jnp.bfloat16)
    local_heads = queries.shape[1]
    local_kv = keys.shape[1]
    head_dim = queries.shape[2]
    head_group = local_heads // local_kv
    score_scale = 1.0 / head_dim**0.5
    grouped_q = queries.reshape(tok_rows, local_kv, head_group, head_dim)

    def update(carried, key_part, value_part, key_start):
        run_max, run_total, run_acc = carried
        count = key_part.shape[0]
        scores = (
            jnp.einsum("tkgd,skd->tkgs", grouped_q, key_part, preferred_element_type=jnp.float32)
            * score_scale
        )
        key_pos = key_start + jnp.arange(count, dtype=jnp.int32)
        allowed = (key_pos[None, :] <= positions[:, None]) & (
            key_pos[None, :] >= req_start[:, None]
        )
        allowed = allowed[:, None, None, :]
        masked = jnp.where(allowed, scores, NEG_FILL)
        new_max = jnp.maximum(run_max, jnp.max(masked, axis=-1))
        expo = jnp.where(allowed, jnp.exp(masked - new_max[..., None]), 0.0)
        rescale = jnp.exp(run_max - new_max)
        weights = expo.astype(jnp.bfloat16)
        run_total = run_total * rescale + jnp.sum(expo, axis=-1)
        products = jnp.einsum(
            "tkgs,skd->tkgd", weights, value_part, preferred_element_type=jnp.float32
        )
        run_acc = run_acc * rescale[..., None] + products
        return (new_max, run_total, run_acc)

    start_state = (
        jnp.full((tok_rows, local_kv, head_group), NEG_FILL, jnp.float32),
        jnp.zeros((tok_rows, local_kv, head_group), jnp.float32),
        jnp.zeros((tok_rows, local_kv, head_group, head_dim), jnp.float32),
    )
    key_piece = lax.all_gather(keys, "seq", axis=0, tiled=True)
    value_piece = lax.all_gather(values, "seq", axis=0, tiled=True)
    count = key_piece.shape[0]
    blocks = count // KEY_BLOCK
    key_blocks = key_piece.reshape(blocks, KEY_BLOCK, local_kv, head_dim)
    value_blocks = value_piece.reshape(blocks, KEY_BLOCK, local_kv, head_dim)

    def block_step(inner_state, item):
        block_index, key_part, value_part = item
        return (update(inner_state, key_part, value_part, block_index * KEY_BLOCK), None)

    final_state, _ = lax.scan(
        block_step, start_state, (jnp.arange(blocks, dtype=jnp.int32), key_blocks, value_blocks)
    )
    final_max, final_total, final_acc = final_state
    context = (
        (final_acc / final_total[..., None])
        .astype(jnp.bfloat16)
        .reshape(tok_rows, local_heads, head_dim)
    )
    partial_bc = jnp.einsum("tc,jc->tj", inner_x, bc_weight, preferred_element_type=jnp.float32)
    summed_bc = lax.psum(partial_bc, "tp")
    state_size = a_log.shape[0]
    b_rows = summed_bc[:, :state_size]
    c_rows = summed_bc[:, state_size:]
    keep_rows = jnp.where(positions == req_start, 0.0, 1.0).astype(jnp.float32)
    rates = jnp.exp(a_log)
    step_sizes = jax.nn.softplus(dt_raw.astype(jnp.float32) + dt_bias[None, :])
    x_float = inner_x.astype(jnp.float32)

    def local_step(carried, item):
        decay_total, state_now = carried
        step_row, x_row, b_row, keep_row = item
        factor = jnp.exp(-step_row[None, :] * rates) * keep_row
        state_now = factor * state_now + (step_row * x_row)[None, :] * b_row[:, None]
        return ((decay_total * factor, state_now), None)

    ones_state = jnp.ones(rates.shape, jnp.float32)
    zero_state = jnp.zeros(rates.shape, jnp.float32)
    (decay_total, end_state), _ = lax.scan(
        local_step, (ones_state, zero_state), (step_sizes, x_float, b_rows, keep_rows), unroll=8
    )
    incoming = prefix((decay_total, end_state), "seq", chain_combine, (ones_state, zero_state))[1]

    def output_step(state_now, item):
        step_row, x_row, b_row, c_row, keep_row = item
        factor = jnp.exp(-step_row[None, :] * rates) * keep_row
        state_now = factor * state_now + (step_row * x_row)[None, :] * b_row[:, None]
        out_row = jnp.sum(c_row[:, None] * state_now, axis=0) + skip_gain * x_row
        return (state_now, out_row.astype(jnp.bfloat16))

    _, mixed = lax.scan(
        output_step, incoming, (step_sizes, x_float, b_rows, c_rows, keep_rows), unroll=8
    )
    return (steered, context, mixed)


def solution(mesh):
    return jax.shard_map(
        shards,
        mesh=mesh,
        in_specs=(
            P("seq", "tp"),
            P(None, "tp"),
            P(),
            P(),
            P(),
            P("seq", "tp", None),
            P("seq", "tp", None),
            P("seq", "tp", None),
            P("seq", "tp"),
            P("seq", "tp"),
            P("tp"),
            P(None, "tp"),
            P("tp"),
            P(None, "tp"),
        ),
        out_specs=(P("seq", "tp"), P("seq", "tp", None), P("seq", "tp")),
        check_vma=False,
    )
```

profile of v0, /device:TPU:504, one launch (start us, length us, event | category | flops | bytes accessed | tf_op | source)
XLA Modules:
  0.0 902.7 jit_solution(4664678258861879669)
XLA Ops:
  13.0 25.6 %psum.7 = f32[128,32]{0,1:T(8,128)S(1)} all-reduce(f32[128,32]{0,1:T(8,128)S(1)} %fusion.102), channel_id=1, replica_groups=mesh['seq'=64,'tp'=8] {'tp'}, use_global_device_ids=true, to_apply=%region_6.7 | all-reduce | flops 4096 | bytes 32768 | tf_op jit(solution)/shard_map/psum | solution.py:123
  39.4 180.9 %while.55 = (s32[]{:T(128)}, f32[16,2048]{1,0:T(8,128)S(1)}, f32[16,2048]{1,0:T(8,128)S(1)}, f32[16,8,2048]{2,1,0:T(8,128)S(1)}, f32[16,2048]{1,0:T(8,128)S(1)},...) while((s32[]{:T(128)}, f32[16,2048]{1,0:T(8,128)S(1)}, ...), condition=%wide.region_8.9_spmd.clone, body=%wide.region_7.8_spmd.clone.sunk | while | flops 2195466 | bytes 1248228 | solution.py:141
  40.3 5.3 fusion.130
  45.6 5.2 fusion.129
  51.6 5.3 fusion.130
  56.9 5.2 fusion.129
  62.9 5.3 fusion.130
  68.2 5.2 fusion.129
  74.2 5.3 fusion.130
  85.5 5.3 fusion.130
  90.8 5.2 fusion.129
  96.8 5.3 fusion.130
  102.1 5.2 fusion.129
  108.2 5.3 fusion.130
  113.4 5.2 fusion.129
  119.5 5.3 fusion.130
  130.8 5.3 fusion.130
  142.1 5.3 fusion.130
  153.4 5.3 fusion.130
  164.7 5.3 fusion.130
  176.0 5.3 fusion.130
  181.3 5.2 fusion.129
  187.3 5.3 fusion.130
  192.6 5.2 fusion.129
  198.6 5.3 fusion.130
  209.9 5.3 fusion.130
  226.1 61.9 %all-gather.9.cloned.1.call-done = bf16[8192,1,128]{2,0,1:T(8,128)(2,1)} async-done(((bf16[128,1,128]{2,0,1:T(8,128)(2,1)}), bf16[8192,1,128]{2,0,1:T(8,128)(2,1)}) %all-gather.9.cloned.1.call-update) | async-done | bytes 2097168 | tf_op jit(solution)/shard_map/all_gather | solution.py:103
  288.1 78.5 %while.54 = (s32[]{:T(128)}, f32[128,1,8]{0,2,1:T(8,128)S(1)}, f32[128,1,8]{0,2,1:T(8,128)S(1)}, f32[128,1,8,128]{0,3,2,1:T(8,128)S(1)}, s32[16]{0:T(128)S(1)}, ...) while((s32[]{:T(128)}, f32[128,1,8]{0,2,1:T(8,128)S(1)}, ...), condition=%wide.region_5.6_spmd.clone, body=%wide.region_2.5_spmd.clone.sunk | while | flops 275847808 | bytes 8198825 | solution.py:113
  367.8 74.9 %all-gather.11.cloned.1.call-done = f32[1024,2048]{1,0:T(8,128)} async-done(((f32[16,2048]{1,0:T(8,128)}), f32[1024,2048]{1,0:T(8,128)}) %all-gather.11.cloned.1.call-update) | async-done | bytes 8388624 | tf_op jit(solution)/shard_map/all_gather | solution.py:12
  442.7 153.9 %all-gather.13.cloned.1.call-done = f32[1024,2048]{1,0:T(8,128)} async-done(((f32[16,2048]{1,0:T(8,128)}), f32[1024,2048]{1,0:T(8,128)}) %all-gather.13.cloned.1.call-update) | async-done | bytes 8388624 | tf_op jit(solution)/shard_map/all_gather | solution.py:12
  596.6 67.0 %while.52 = (s32[]{:T(128)}, f32[16,2048]{1,0:T(8,128)S(1)}, s32[]{:T(128)}, f32[64,16,2048]{2,1,0:T(8,128)}, f32[64,16,2048]{2,1,0:T(8,128)}, /*index=5*/s32[]{:T(128)}, s32[]{:T(128)}, s32[]{:T(128)}) while((s32[]{:T(128)}, f32[16,2048]{1,0:T(8,128)S(1)}, s32[]{:T(128)}, f32[64,16,2048]{2,1,0:T(8,128)}, f32[64,16,2048]{2,1,0:T(8,128)}, ...), condition=%wide.region_10.11_spmd, body=%wide.region_9.10_spmd.sunk | while | flops 65541 | bytes 524411 | solution.py:20
  663.6 232.7 %while.53 = (s32[]{:T(128)}, f32[16,2048]{1,0:T(8,128)S(1)}, bf16[16,8,2048]{2,1,0:T(8,128)(2,1)}, f32[16,8,2048]{2,1,0:T(8,128)}, f32[16,2048]{1,0:T(8,128)S(1)...) while((s32[]{:T(128)}, f32[16,2048]{1,0:T(8,128)S(1)}, ...), condition=%wide.region_20.21_spmd, body=%wide.region_11.20_spmd.sunk | while | flops 2883593 | bytes 1915265 | solution.py:153
  (565 shorter events, 434.1 us)
Async XLA Ops:
  7.2 4.5 copy-start
  7.2 31.6 %copy-start.8 = (f32[16,2048]{1,0:T(8,128)S(1)}, f32[16,2048]{1,0:T(8,128)}, u32[]{:S(2)}) copy-start(f32[16,2048]{1,0:T(8,128)} %param.33) | copy-start | bytes 393220
  7.2 31.6 %copy-start.4 = (bf16[128,2048]{1,0:T(8,128)(2,1)S(1)}, bf16[128,2048]{1,0:T(8,128)(2,1)}, u32[]{:S(2)}) copy-start(bf16[128,2048]{1,0:T(8,128)(2,1)} %param.31) | copy-start | bytes 1572868
  7.2 31.6 %copy-start.10 = (f32[2048]{0:T(1024)S(1)}, f32[2048]{0:T(1024)}, u32[]{:S(2)}) copy-start(f32[2048]{0:T(1024)} %param.32) | copy-start | bytes 24580
  7.2 218.9 %all-gather.7.cloned.1.call-start = ((), (), s32[]{:S(2)}) async-start(), calls=%async_computation | async-start | bytes 2129920 | tf_op jit(solution)/shard_map/all_gather | solution.py:102
  7.9 280.1 %all-gather.9.cloned.1.call-start = ((), (), s32[]{:S(2)}) async-start(), calls=%async_computation.1 | async-start | bytes 2129920 | tf_op jit(solution)/shard_map/all_gather | solution.py:103
  8.7 434.0 %all-gather.11.cloned.1.call-start = ((), (), s32[]{:S(2)}) async-start(), calls=%async_computation.2 | async-start | bytes 8519680 | tf_op jit(solution)/shard_map/all_gather | solution.py:12
  10.3 2.7 copy-start.11
  39.4 183.0 %copy-start.5 = (bf16[128,8,128]{2,1,0:T(8,128)(2,1)S(1)}, bf16[128,8,128]{2,1,0:T(8,128)(2,1)}, u32[]{:S(2)}) copy-start(bf16[128,8,128]{2,1,0:T(8,128)(2,1)} %param.27) | copy-start | bytes 786436
  220.3 0.7 copy-start.9
  220.4 0.7 copy-start.1
  220.4 1.3 copy-start.7
  220.4 67.7 %copy-start.2 = (f32[16,8,2048]{2,1,0:T(8,128)}, f32[16,8,2048]{2,1,0:T(8,128)S(1)}, u32[]{:S(2)}) copy-start(f32[16,8,2048]{2,1,0:T(8,128)S(1)} %get-tuple-element.1075) | copy-start | bytes 3145732
  220.4 67.7 %copy-start.3 = (f32[16,8,2048]{2,1,0:T(8,128)}, f32[16,8,2048]{2,1,0:T(8,128)S(1)}, u32[]{:S(2)}) copy-start(f32[16,8,2048]{2,1,0:T(8,128)S(1)} %get-tuple-element.1076) | copy-start | bytes 3145732
  221.0 375.5 %all-gather.13.cloned.1.call-start = ((), (), s32[]{:S(2)}) async-start(), calls=%async_computation.3 | async-start | bytes 8519680 | tf_op jit(solution)/shard_map/all_gather | solution.py:12
  366.8 296.7 %copy-start.6 = (f32[2048]{0:T(1024)S(1)}, f32[2048]{0:T(1024)}, u32[]{:S(2)}) copy-start(f32[2048]{0:T(1024)} %param.34) | copy-start | bytes 24580
Sparse Core Ops, SparseCore 0:
  11.0 137.2 all-gather.6
  151.2 136.8 all-gather.8
  291.0 151.6 all-gather.10
  445.5 151.0 all-gather.12
where the time goes:
time: 912 us; the launch traced here: 903 us
  other arithmetic  449 us (49%)
  waiting for transfers between devices  293 us (32%)
  local copies, waits for them, and re-layouts  56.6 us (6%)
  matrix products  52.2 us (6%)
  blocking collectives  25.6 us (3%)
  between operations  14.1 us (2%)
  loops' own time  12.7 us (1%)
    all_gather x2, waiting for transfers between devices, prefix(): gathered = jax.tree.map(lambda a: lax.all_gather(a, axis), part)  229 us
    reduce_sum x48, other arithmetic, output_step(): out_row = jnp.sum(c_row[:, None] * state_now, axis=0) + skip_gain * x_row  147 us
    add x16, other arithmetic, local_step(): factor * state_now + (step_row * x_row)[None, :] * b_row[:, None]  84.3 us
    mul x16, other arithmetic, local_step(): return ((decay_total * factor, state_now), None)  82.6 us
    add x63, other arithmetic, chain_combine(): return (earlier[0] * later[0], later[0] * earlier[1] + later[1])  65.4 us
    all_gather x1, waiting for transfers between devices, shards(): value_piece = lax.all_gather(values, 'seq', axis=0, tiled=True)  61.9 us
    mul x16, other arithmetic, output_step(): step_row * x_row  29.2 us
    dot_general x16, matrix products, update(): jnp.einsum('tkgs,skd->tkgd', weights, value_part, preferred_element_type=...  26 us
  transfers between devices with their start and end apart: 4, of which 3 were waited for; matrix products, arithmetic and copies ran while one was open for 29% of the time, Pallas kernels for 0%

commit v1 on v0

--- a/solution.py
+++ b/solution.py
@@ -120,7 +120,7 @@
         .reshape(tok_rows, local_heads, head_dim)
     )
     partial_bc = jnp.einsum("tc,jc->tj", inner_x, bc_weight, preferred_element_type=jnp.float32)
-    summed_bc = lax.psum(partial_bc, "tp")
+    summed_bc = lax.all_gather(partial_bc, "tp").sum(axis=0)
     state_size = a_log.shape[0]
     b_rows = summed_bc[:, :state_size]
     c_rows = summed_bc[:, state_size:]

time: 912 us -> 912 us (level)
  blocking collectives: 25.6 us -> 13.1 us
  waiting for transfers between devices: 293 us -> 305 us
    psum x1 -> x0, blocking collectives: 25.6 us -> none  [shards(): summed_bc = lax.psum(partial_bc, 'tp')]
    all_gather x0 -> x1, blocking collectives: none -> 13.1 us  [shards(): summed_bc = lax.all_gather(partial_bc, 'tp').sum(axis=0)]
    all_gather x1, waiting for transfers between devices: 61.9 us -> 74.4 us  [shards(): value_piece = lax.all_gather(values, 'seq', axis=0, tiled=True)]
where the time goes in v1:
time: 912 us; the launch traced here: 903 us
  other arithmetic  449 us (49%)
  waiting for transfers between devices  305 us (33%)
  local copies, waits for them, and re-layouts  56.6 us (6%)
  matrix products  52.2 us (6%)
  between operations  14.1 us (2%)
  blocking collectives  13.1 us (1%)
  loops' own time  12.7 us (1%)
    all_gather x2, waiting for transfers between devices, prefix(): gathered = jax.tree.map(lambda a: lax.all_gather(a, axis), part)  229 us
    reduce_sum x48, other arithmetic, output_step(): out_row = jnp.sum(c_row[:, None] * state_now, axis=0) + skip_gain * x_row  147 us
    add x16, other arithmetic, local_step(): factor * state_now + (step_row * x_row)[None, :] * b_row[:, None]  84.3 us
    mul x16, other arithmetic, local_step(): return ((decay_total * factor, state_now), None)  82.6 us
    all_gather x1, waiting for transfers between devices, shards(): value_piece = lax.all_gather(values, 'seq', axis=0, tiled=True)  74.4 us
    add x63, other arithmetic, chain_combine(): return (earlier[0] * later[0], later[0] * earlier[1] + later[1])  65.3 us
    mul x16, other arithmetic, output_step(): step_row * x_row  29.2 us
    dot_general x16, matrix products, update(): jnp.einsum('tkgs,skd->tkgd', weights, value_part, preferred_element_type=...  26 us
  transfers between devices with their start and end apart: 4, of which 3 were waited for; matrix products, arithmetic and copies ran while one was open for 29% of the time, Pallas kernels for 0%

profile of v1, /device:TPU:504, one launch (start us, length us, event | category | flops | bytes accessed | tf_op | source)
XLA Modules:
  0.0 902.7 jit_solution(5922571319332164940)
XLA Ops:
  13.0 13.1 %all-gather = f32[1024,32]{0,1:T(8,128)S(1)} all-gather(f32[128,32]{0,1:T(8,128)S(1)} %fusion.102), channel_id=2, replica_groups=mesh['seq'=64,'tp'=8] {'tp'}, dimensions={0}, use_global_device_ids=true | all-gather | bytes 147456 | tf_op jit(solution)/shard_map/all_gather | solution.py:123
  27.0 180.9 %while.55 = (s32[]{:T(128)}, f32[16,2048]{1,0:T(8,128)S(1)}, f32[16,2048]{1,0:T(8,128)S(1)}, f32[16,8,2048]{2,1,0:T(8,128)S(1)}, f32[16,2048]{1,0:T(8,128)S(1)},...) while((s32[]{:T(128)}, f32[16,2048]{1,0:T(8,128)S(1)}, ...), condition=%wide.region_8.9_spmd.clone, body=%wide.region_7.8_spmd.clone.sunk | while | flops 2195466 | bytes 1248228 | solution.py:141
  27.9 5.3 fusion.130
  33.2 5.2 fusion.129
  39.2 5.3 fusion.130
  44.5 5.2 fusion.129
  50.5 5.3 fusion.130
  55.8 5.2 fusion.129
  61.8 5.3 fusion.130
  73.1 5.3 fusion.130
  78.4 5.2 fusion.129
  84.4 5.3 fusion.130
  89.7 5.2 fusion.129
  95.7 5.3 fusion.130
  107.0 5.3 fusion.130
  118.3 5.3 fusion.130
  129.6 5.3 fusion.130
  134.9 5.2 fusion.129
  141.0 5.3 fusion.130
  152.3 5.3 fusion.130
  163.6 5.3 fusion.130
  174.9 5.3 fusion.130
  180.1 5.2 fusion.129
  186.2 5.3 fusion.130
  191.4 5.2 fusion.129
  197.5 5.3 fusion.130
  213.7 74.4 %all-gather.10.cloned.1.call-done = bf16[8192,1,128]{2,0,1:T(8,128)(2,1)} async-done(((bf16[128,1,128]{2,0,1:T(8,128)(2,1)}), bf16[8192,1,128]{2,0,1:T(8,128)(2,1)}) %all-gather.10.cloned.1.call-update) | async-done | bytes 2097168 | tf_op jit(solution)/shard_map/all_gather | solution.py:103
  288.1 78.5 %while.54 = (s32[]{:T(128)}, f32[128,1,8]{0,2,1:T(8,128)S(1)}, f32[128,1,8]{0,2,1:T(8,128)S(1)}, f32[128,1,8,128]{0,3,2,1:T(8,128)S(1)}, s32[16]{0:T(128)S(1)}, ...) while((s32[]{:T(128)}, f32[128,1,8]{0,2,1:T(8,128)S(1)}, ...), condition=%wide.region_5.6_spmd.clone, body=%wide.region_2.5_spmd.clone.sunk | while | flops 275847808 | bytes 8198825 | solution.py:113
  367.8 74.9 %all-gather.12.cloned.1.call-done = f32[1024,2048]{1,0:T(8,128)} async-done(((f32[16,2048]{1,0:T(8,128)}), f32[1024,2048]{1,0:T(8,128)}) %all-gather.12.cloned.1.call-update) | async-done | bytes 8388624 | tf_op jit(solution)/shard_map/all_gather | solution.py:12
  442.7 153.9 %all-gather.14.cloned.1.call-done = f32[1024,2048]{1,0:T(8,128)} async-done(((f32[16,2048]{1,0:T(8,128)}), f32[1024,2048]{1,0:T(8,128)}) %all-gather.14.cloned.1.call-update) | async-done | bytes 8388624 | tf_op jit(solution)/shard_map/all_gather | solution.py:12
  596.6 66.9 %while.52 = (s32[]{:T(128)}, f32[16,2048]{1,0:T(8,128)S(1)}, s32[]{:T(128)}, f32[64,16,2048]{2,1,0:T(8,128)}, f32[64,16,2048]{2,1,0:T(8,128)}, /*index=5*/s32[]{:T(128)}, s32[]{:T(128)}, s32[]{:T(128)}) while((s32[]{:T(128)}, f32[16,2048]{1,0:T(8,128)S(1)}, s32[]{:T(128)}, f32[64,16,2048]{2,1,0:T(8,128)}, f32[64,16,2048]{2,1,0:T(8,128)}, ...), condition=%wide.region_10.11_spmd, body=%wide.region_9.10_spmd.sunk | while | flops 65541 | bytes 524411 | solution.py:20
  663.5 232.7 %while.53 = (s32[]{:T(128)}, f32[16,2048]{1,0:T(8,128)S(1)}, bf16[16,8,2048]{2,1,0:T(8,128)(2,1)}, f32[16,8,2048]{2,1,0:T(8,128)}, f32[16,2048]{1,0:T(8,128)S(1)...) while((s32[]{:T(128)}, f32[16,2048]{1,0:T(8,128)S(1)}, ...), condition=%wide.region_20.21_spmd, body=%wide.region_11.20_spmd.sunk | while | flops 2883593 | bytes 1915265 | solution.py:153
  (567 shorter events, 434.1 us)
Async XLA Ops:
  7.2 4.5 copy-start
  7.2 19.1 %copy-start.8 = (f32[16,2048]{1,0:T(8,128)S(1)}, f32[16,2048]{1,0:T(8,128)}, u32[]{:S(2)}) copy-start(f32[16,2048]{1,0:T(8,128)} %param.33) | copy-start | bytes 393220
  7.2 19.2 %copy-start.4 = (bf16[128,2048]{1,0:T(8,128)(2,1)S(1)}, bf16[128,2048]{1,0:T(8,128)(2,1)}, u32[]{:S(2)}) copy-start(bf16[128,2048]{1,0:T(8,128)(2,1)} %param.31) | copy-start | bytes 1572868
  7.2 19.2 %copy-start.10 = (f32[2048]{0:T(1024)S(1)}, f32[2048]{0:T(1024)}, u32[]{:S(2)}) copy-start(f32[2048]{0:T(1024)} %param.32) | copy-start | bytes 24580
  7.2 206.5 %all-gather.8.cloned.1.call-start = ((), (), s32[]{:S(2)}) async-start(), calls=%async_computation | async-start | bytes 2129920 | tf_op jit(solution)/shard_map/all_gather | solution.py:102
  7.9 280.1 %all-gather.10.cloned.1.call-start = ((), (), s32[]{:S(2)}) async-start(), calls=%async_computation.1 | async-start | bytes 2129920 | tf_op jit(solution)/shard_map/all_gather | solution.py:103
  8.7 434.0 %all-gather.12.cloned.1.call-start = ((), (), s32[]{:S(2)}) async-start(), calls=%async_computation.2 | async-start | bytes 8519680 | tf_op jit(solution)/shard_map/all_gather | solution.py:12
  10.3 15.9 %copy-start.11 = (s32[4]{0:T(128)}, s32[4]{0:T(128)S(1)}, u32[]{:S(2)}) copy-start(s32[4]{0:T(128)S(1)} %bitcast_subtract_fusion) | copy-start | bytes 52
  27.0 183.0 %copy-start.5 = (bf16[128,8,128]{2,1,0:T(8,128)(2,1)S(1)}, bf16[128,8,128]{2,1,0:T(8,128)(2,1)}, u32[]{:S(2)}) copy-start(bf16[128,8,128]{2,1,0:T(8,128)(2,1)} %param.27) | copy-start | bytes 786436
  207.9 0.7 copy-start.9
  207.9 0.7 copy-start.1
  207.9 1.3 copy-start.7
  208.0 80.1 %copy-start.2 = (f32[16,8,2048]{2,1,0:T(8,128)}, f32[16,8,2048]{2,1,0:T(8,128)S(1)}, u32[]{:S(2)}) copy-start(f32[16,8,2048]{2,1,0:T(8,128)S(1)} %get-tuple-element.1131) | copy-start | bytes 3145732
  208.0 80.1 %copy-start.3 = (f32[16,8,2048]{2,1,0:T(8,128)}, f32[16,8,2048]{2,1,0:T(8,128)S(1)}, u32[]{:S(2)}) copy-start(f32[16,8,2048]{2,1,0:T(8,128)S(1)} %get-tuple-element.1132) | copy-start | bytes 3145732
  208.6 388.0 %all-gather.14.cloned.1.call-start = ((), (), s32[]{:S(2)}) async-start(), calls=%async_computation.3 | async-start | bytes 8519680 | tf_op jit(solution)/shard_map/all_gather | solution.py:12
  366.8 296.7 %copy-start.6 = (f32[2048]{0:T(1024)S(1)}, f32[2048]{0:T(1024)}, u32[]{:S(2)}) copy-start(f32[2048]{0:T(1024)} %param.34) | copy-start | bytes 24580
Sparse Core Ops, SparseCore 0:
  11.0 137.1 all-gather.7
  151.1 136.9 all-gather.9
  291.0 151.6 all-gather.11
  445.5 151.0 all-gather.13
